TPU v7x, 32 devices: a whole 2x2x4 slice. The times are simulated.
32 devices in a mesh: dp: 8 (over z, x), tensor: 4 (over y, core).
Axes of the slice: x: 2, y: 2, z: 4, core: 2. Of those that a mesh axis runs over, the one named last changes fastest.
Arguments:
- tokens: bfloat16 [16384, 1024], P(('dp', 'tensor')), may hold values from -6 to 6
- cotangent: bfloat16 [16384, 1024], P(('dp', 'tensor')), may hold values from -6 to 6
- lengths: int32 [8, 16], P('dp'), may hold values from 1 to 256, 2048 in all within a row
- qkv_master: float32 [1024, 3, 1024], P('dp', None, 'tensor'), may hold values from -0.1875 to 0.1875
- qkv_first: float32 [1024, 3, 1024], P('dp', None, 'tensor'), may hold values from -0.00015258789 to 0.00015258789
- qkv_second: float32 [1024, 3, 1024], P('dp', None, 'tensor'), may hold values from 2.9798684e-11 to 4.7677895e-10
- out_master: float32 [1024, 1024], P(('tensor', 'dp')), may hold values from -1 to 1
- out_first: float32 [1024, 1024], P(('tensor', 'dp')), may hold values from -9.1552734e-05 to 9.1552734e-05
- out_second: float32 [1024, 1024], P(('tensor', 'dp')), may hold values from 5.959737e-12 to 9.535579e-11
- in_master: float32 [1024, 2, 4096], P('dp', None, 'tensor'), may hold values from -0.1875 to 0.1875
- in_first: float32 [1024, 2, 4096], P('dp', None, 'tensor'), may hold values from -0.00015258789 to 0.00015258789
- in_second: float32 [1024, 2, 4096], P('dp', None, 'tensor'), may hold values from 2.9798684e-11 to 4.7677895e-10
- down_master: float32 [4096, 1024], P(('tensor', 'dp')), may hold values from -0.09375 to 0.09375
- down_first: float32 [4096, 1024], P(('tensor', 'dp')), may hold values from -0.00015258789 to 0.00015258789
- down_second: float32 [4096, 1024], P(('tensor', 'dp')), may hold values from 2.9798684e-11 to 4.7677895e-10
- norm_gains: float32 [2, 1024], replicated, may hold values from 0.2 to 2.8
- gain_first: float32 [2, 1024], replicated, may hold values from -0.00061035156 to 0.00061035156
- gain_second: float32 [2, 1024], replicated, may hold values from 4.7677895e-10 to 7.628463e-09
Outputs:
- layer_out: bfloat16 [16384, 1024], P(('dp', 'tensor'))
- input_grad: float32 [16384, 1024], P(('dp', 'tensor'))
- qkv_grad: float32 [1024, 3, 1024], P('dp', None, 'tensor')
- qkv_new: float32 [1024, 3, 1024], P('dp', None, 'tensor')
- qkv_first_new: float32 [1024, 3, 1024], P('dp', None, 'tensor')
- qkv_second_new: float32 [1024, 3, 1024], P('dp', None, 'tensor')
- out_grad: float32 [1024, 1024], P(('tensor', 'dp'))
- out_new: float32 [1024, 1024], P(('tensor', 'dp'))
- out_first_new: float32 [1024, 1024], P(('tensor', 'dp'))
- out_second_new: float32 [1024, 1024], P(('tensor', 'dp'))
- in_grad: float32 [1024, 2, 4096], P('dp', None, 'tensor')
- in_new: float32 [1024, 2, 4096], P('dp', None, 'tensor')
- in_first_new: float32 [1024, 2, 4096], P('dp', None, 'tensor')
- in_second_new: float32 [1024, 2, 4096], P('dp', None, 'tensor')
- down_grad: float32 [4096, 1024], P(('tensor', 'dp'))
- down_new: float32 [4096, 1024], P(('tensor', 'dp'))
- down_first_new: float32 [4096, 1024], P(('tensor', 'dp'))
- down_second_new: float32 [4096, 1024], P(('tensor', 'dp'))
- gain_grad: float32 [2, 1024], replicated
- gain_new: float32 [2, 1024], replicated
- gain_first_new: float32 [2, 1024], replicated
- gain_second_new: float32 [2, 1024], replicated
- grad_norm: float32 [], replicated
Inputs may be any that keep to these rules, and one draw needn't show every extreme that they name: Each row's 16 window lengths are positive, add up to 2048, and the longest is 256.
All inputs are finite; a program needn't handle non-finite values.
Results may differ from a plain program's by a relative error of at most 0.024.
Values may be sent and summed in bfloat16 or wider, within the bound.
No kernel may reach another device: no remote copies, remote signals or barrier semaphores. Data moves between devices by JAX's collectives and lax.ppermute only.
A program may use at most 192 MiB of HBM per device.

v0:
```python
from functools import partial
import math
import jax
import jax.numpy as jnp
from jax import lax
from jax.sharding import PartitionSpec as P

D = 1024
HEADS = 16
HEAD_DIM = 64
FF = 4096
ROW = 2048
STEP = 5
eps_norm = 1e-05
beta_one = 0.9
beta_two = 0.999
learn_rate = 0.05
gain_rate = 0.6
weight_decay = 0.1
adam_eps = 1e-08
max_norm = 1.0


def layer_norm(values, gain):
    centre = values - jnp.mean(values, axis=-1, keepdims=True)
    spread = jnp.mean(centre * centre, axis=-1, keepdims=True)
    return centre * lax.rsqrt(spread + eps_norm) * gain


def row_layout(lengths):
    seg_ends = jnp.cumsum(lengths, axis=-1)
    places = jnp.arange(ROW, dtype=jnp.int32)
    passed = (places[:, None] >= seg_ends[..., None, :]).astype(jnp.int32)
    segment = jnp.sum(passed, axis=-1)
    offset = places - jnp.sum(passed * lengths[..., None, :], axis=-1)
    return (segment, offset)


def rotary_tables(offset):
    half_dim = HEAD_DIM // 2
    inverse = jnp.exp(
        jnp.arange(half_dim, dtype=jnp.float32) * (-2.0 * math.log(10000.0) / HEAD_DIM)
    )
    angles = offset.astype(jnp.float32)[..., None] * inverse
    return (jnp.cos(angles), jnp.sin(angles))


def rotate(values, cosine, sine):
    half_dim = values.shape[-1] // 2
    front_half = values[..., :half_dim]
    back_half = values[..., half_dim:]
    cos_wide = cosine[..., None, :]
    sin_wide = sine[..., None, :]
    return jnp.concatenate(
        [
            front_half * cos_wide - back_half * sin_wide,
            back_half * cos_wide + front_half * sin_wide,
        ],
        axis=-1,
    )


def swiglu(gate_up):
    half_cols = gate_up.shape[-1] // 2
    return jax.nn.silu(gate_up[:, :half_cols]) * gate_up[:, half_cols:]


def adam_update(weight, first_moment, second_moment, gradient, factor, use_decay, rate):
    clipped = gradient * factor
    first_new = beta_one * first_moment + (1.0 - beta_one) * clipped
    second_new = beta_two * second_moment + (1.0 - beta_two) * clipped * clipped
    first_hat = first_new / (1.0 - beta_one**STEP)
    second_hat = second_new / (1.0 - beta_two**STEP)
    direction = first_hat / (jnp.sqrt(second_hat) + adam_eps) + use_decay * weight_decay * weight
    return (clipped, weight - rate * direction, first_new, second_new)


def contract_rows(left, right):
    return lax.dot_general(
        left, right, (((0,), (0,)), ((), ())), preferred_element_type=jnp.float32
    )


def contract_cols(left, right):
    return lax.dot_general(
        left, right, (((1,), (1,)), ((), ())), preferred_element_type=jnp.float32
    )


def per_device(
    tokens,
    cotangent,
    lengths,
    qkv_master,
    qkv_first,
    qkv_second,
    out_master,
    out_first,
    out_second,
    in_master,
    in_first,
    in_second,
    down_master,
    down_first,
    down_second,
    norm_gains,
    gain_first,
    gain_second,
):
    heads_local = HEADS // lax.axis_size("tensor")
    width_local = heads_local * HEAD_DIM
    ffn_local = FF // lax.axis_size("tensor")
    row_count = lengths.shape[0]
    all_rows = row_count * ROW
    score_scale = HEAD_DIM ** (-0.5)
    block_rows = min(512, ROW)
    block_count = ROW // block_rows
    w_qkv, w_out, w_in, w_down = (
        lax.all_gather(qkv_master.astype(jnp.bfloat16), "dp", axis=0, tiled=True),
        lax.all_gather(out_master.astype(jnp.bfloat16), "dp", axis=0, tiled=True),
        lax.all_gather(in_master.astype(jnp.bfloat16), "dp", axis=0, tiled=True),
        lax.all_gather(down_master.astype(jnp.bfloat16), "dp", axis=0, tiled=True),
    )
    w_qkv = w_qkv.reshape(D, 3 * width_local)
    w_in = w_in.reshape(D, 2 * ffn_local)
    segment, offset = row_layout(lengths)
    cosine, sine = rotary_tables(offset)
    gain_one = norm_gains[0]
    gain_two = norm_gains[1]
    inputs = tokens.astype(jnp.float32)
    normed = layer_norm(inputs, gain_one)
    gathered_one = lax.all_gather(normed.astype(jnp.bfloat16), "tensor", axis=0, tiled=True)
    projected = jnp.dot(gathered_one, w_qkv, preferred_element_type=jnp.float32)
    projected = projected.reshape(row_count, ROW, 3, heads_local, HEAD_DIM)
    queries = rotate(projected[:, :, 0], cosine, sine).astype(jnp.bfloat16)
    keys = rotate(projected[:, :, 1], cosine, sine).astype(jnp.bfloat16)
    values = projected[:, :, 2].astype(jnp.bfloat16)

    def score_block(query_block, key_row, segment_block, segment_row):
        scores = (
            jnp.einsum("qhd,khd->hqk", query_block, key_row, preferred_element_type=jnp.float32)
            * score_scale
        )
        allowed = segment_block[:, None] == segment_row[None, :]
        return jnp.where(allowed[None], scores, -1e30)

    def forward_row(pieces):
        query_row, key_row, value_row, segment_row = pieces

        def forward_block(block_parts):
            query_block, segment_block = block_parts
            masked = score_block(query_block, key_row, segment_block, segment_row)
            row_max = jnp.max(masked, axis=-1, keepdims=True)
            log_total = (
                jnp.log(jnp.sum(jnp.exp(masked - row_max), axis=-1, keepdims=True)) + row_max
            )
            weights = jnp.exp(masked - log_total).astype(jnp.bfloat16)
            mixed_heads = jnp.einsum(
                "hqk,khd->qhd", weights, value_row, preferred_element_type=jnp.float32
            )
            return (mixed_heads.astype(jnp.bfloat16), log_total)

        return lax.map(
            forward_block,
            (
                query_row.reshape(block_count, block_rows, heads_local, HEAD_DIM),
                segment_row.reshape(block_count, block_rows),
            ),
        )

    mixed_heads, log_totals = lax.map(forward_row, (queries, keys, values, segment))
    attended = mixed_heads.reshape(all_rows, width_local)
    middle = inputs + lax.psum_scatter(
        jnp.dot(attended, w_out, preferred_element_type=jnp.float32),
        "tensor",
        scatter_dimension=0,
        tiled=True,
    )
    normed_two = layer_norm(middle, gain_two)
    gathered_two = lax.all_gather(normed_two.astype(jnp.bfloat16), "tensor", axis=0, tiled=True)
    gate_up = jnp.dot(gathered_two, w_in, preferred_element_type=jnp.float32)
    hidden = swiglu(gate_up).astype(jnp.bfloat16)
    output = middle + lax.psum_scatter(
        jnp.dot(hidden, w_down, preferred_element_type=jnp.float32).astype(jnp.bfloat16),
        "tensor",
        scatter_dimension=0,
        tiled=True,
    ).astype(jnp.float32)
    layer_out = output.astype(jnp.bfloat16)
    upstream = cotangent.astype(jnp.float32)
    gathered_down = lax.all_gather(cotangent, "tensor", axis=0, tiled=True)
    grad_down = contract_rows(hidden, gathered_down)
    hidden_grad = contract_cols(gathered_down, w_down)
    gate_up_grad = jax.vjp(swiglu, gate_up)[1](hidden_grad)[0].astype(jnp.bfloat16)
    grad_in = contract_rows(gathered_two, gate_up_grad)
    normed_two_grad = lax.psum_scatter(
        contract_cols(gate_up_grad, w_in).astype(jnp.bfloat16),
        "tensor",
        scatter_dimension=0,
        tiled=True,
    ).astype(jnp.float32)
    middle_back, gain_two_grad = jax.vjp(layer_norm, middle, gain_two)[1](normed_two_grad)
    middle_grad = upstream + middle_back
    gathered_mid = lax.all_gather(middle_grad.astype(jnp.bfloat16), "tensor", axis=0, tiled=True)
    grad_out = contract_rows(attended, gathered_mid)
    attended_grad = contract_cols(gathered_mid, w_out).astype(jnp.bfloat16)
    attended_grad = attended_grad.reshape(row_count, ROW, heads_local, HEAD_DIM)

    def backward_row(pieces):
        query_row, key_row, value_row, segment_row, total_row, grad_row = pieces

        def backward_block(running, block_parts):
            key_acc, value_acc = running
            query_block, segment_block, total_block, grad_block = block_parts
            masked = score_block(query_block, key_row, segment_block, segment_row)
            probs_block = jnp.exp(masked - total_block)
            probs_low = probs_block.astype(jnp.bfloat16)
            prob_grad = jnp.einsum(
                "qhd,khd->hqk", grad_block, value_row, preferred_element_type=jnp.float32
            )
            row_inner = jnp.sum(probs_block * prob_grad, axis=-1, keepdims=True)
            score_grad = (probs_block * (prob_grad - row_inner)).astype(jnp.bfloat16)
            query_grad = (
                jnp.einsum("hqk,khd->qhd", score_grad, key_row, preferred_element_type=jnp.float32)
                * score_scale
            )
            key_acc = (
                key_acc
                + jnp.einsum(
                    "hqk,qhd->khd", score_grad, query_block, preferred_element_type=jnp.float32
                )
                * score_scale
            )
            value_acc = value_acc + jnp.einsum(
                "hqk,qhd->khd", probs_low, grad_block, preferred_element_type=jnp.float32
            )
            return ((key_acc, value_acc), query_grad)

        zeros_acc = jnp.zeros((ROW, heads_local, HEAD_DIM), jnp.float32)
        block_inputs = (
            query_row.reshape(block_count, block_rows, heads_local, HEAD_DIM),
            segment_row.reshape(block_count, block_rows),
            total_row,
            grad_row.reshape(block_count, block_rows, heads_local, HEAD_DIM),
        )
        (key_grad, value_grad), query_grad = lax.scan(
            backward_block, (zeros_acc, zeros_acc), block_inputs
        )
        return (query_grad.reshape(ROW, heads_local, HEAD_DIM), key_grad, value_grad)

    query_grad, key_grad, value_grad = lax.map(
        backward_row, (queries, keys, values, segment, log_totals, attended_grad)
    )
    rotate_back = jax.vjp(partial(rotate, cosine=cosine, sine=sine), projected[:, :, 0])[1]
    query_raw = rotate_back(query_grad)[0]
    key_raw = rotate_back(key_grad)[0]
    qkv_grad_low = (
        jnp.stack([query_raw, key_raw, value_grad], axis=2)
        .reshape(all_rows, 3 * width_local)
        .astype(jnp.bfloat16)
    )
    grad_qkv = contract_rows(gathered_one, qkv_grad_low)
    normed_grad = lax.psum_scatter(
        contract_cols(qkv_grad_low, w_qkv).astype(jnp.bfloat16),
        "tensor",
        scatter_dimension=0,
        tiled=True,
    ).astype(jnp.float32)
    input_back, gain_one_grad = jax.vjp(layer_norm, inputs, gain_one)[1](normed_grad)
    input_grad = middle_grad + input_back
    reduced_qkv, reduced_out, reduced_in, reduced_down = (
        lax.psum_scatter(
            grad_qkv.reshape(D, 3, width_local).astype(jnp.bfloat16),
            "dp",
            scatter_dimension=0,
            tiled=True,
        ).astype(jnp.float32),
        lax.psum_scatter(
            grad_out.astype(jnp.bfloat16), "dp", scatter_dimension=0, tiled=True
        ).astype(jnp.float32),
        lax.psum_scatter(
            grad_in.reshape(D, 2, ffn_local).astype(jnp.bfloat16),
            "dp",
            scatter_dimension=0,
            tiled=True,
        ).astype(jnp.float32),
        lax.psum_scatter(
            grad_down.astype(jnp.bfloat16), "dp", scatter_dimension=0, tiled=True
        ).astype(jnp.float32),
    )
    local_squares = (
        jnp.sum(reduced_qkv * reduced_qkv)
        + jnp.sum(reduced_out * reduced_out)
        + jnp.sum(reduced_in * reduced_in)
        + jnp.sum(reduced_down * reduced_down)
    )
    gain_part = jnp.stack([gain_one_grad, gain_two_grad])
    gain_total, weight_squares = lax.psum((gain_part, local_squares), ("dp", "tensor"))
    grad_norm = jnp.sqrt(weight_squares + jnp.sum(gain_total * gain_total))
    factor = max_norm / jnp.maximum(grad_norm, max_norm)
    qkv_res = adam_update(qkv_master, qkv_first, qkv_second, reduced_qkv, factor, 1.0, learn_rate)
    out_res = adam_update(out_master, out_first, out_second, reduced_out, factor, 1.0, learn_rate)
    in_res = adam_update(in_master, in_first, in_second, reduced_in, factor, 1.0, learn_rate)
    down_res = adam_update(
        down_master, down_first, down_second, reduced_down, factor, 1.0, learn_rate
    )
    gain_res = adam_update(norm_gains, gain_first, gain_second, gain_total, factor, 0.0, gain_rate)
    return (
        layer_out,
        input_grad,
        qkv_res[0],
        qkv_res[1],
        qkv_res[2],
        qkv_res[3],
        out_res[0],
        out_res[1],
        out_res[2],
        out_res[3],
        in_res[0],
        in_res[1],
        in_res[2],
        in_res[3],
        down_res[0],
        down_res[1],
        down_res[2],
        down_res[3],
        gain_res[0],
        gain_res[1],
        gain_res[2],
        gain_res[3],
        grad_norm,
    )


def solution(mesh):
    placed = (
        P(("dp", "tensor"), None),
        P(("dp", "tensor"), None),
        P("dp", None),
        P("dp", None, "tensor"),
        P("dp", None, "tensor"),
        P("dp", None, "tensor"),
        P(("tensor", "dp"), None),
        P(("tensor", "dp"), None),
        P(("tensor", "dp"), None),
        P("dp", None, "tensor"),
        P("dp", None, "tensor"),
        P("dp", None, "tensor"),
        P(("tensor", "dp"), None),
        P(("tensor", "dp"), None),
        P(("tensor", "dp"), None),
        P(),
        P(),
        P(),
    )
    return jax.shard_map(
        per_device,
        mesh=mesh,
        in_specs=placed,
        out_specs=(
            P(("dp", "tensor"), None),
            P(("dp", "tensor"), None),
            P("dp", None, "tensor"),
            P("dp", None, "tensor"),
            P("dp", None, "tensor"),
            P("dp", None, "tensor"),
            P(("tensor", "dp"), None),
            P(("tensor", "dp"), None),
            P(("tensor", "dp"), None),
            P(("tensor", "dp"), None),
            P("dp", None, "tensor"),
            P("dp", None, "tensor"),
            P("dp", None, "tensor"),
            P("dp", None, "tensor"),
            P(("tensor", "dp"), None),
            P(("tensor", "dp"), None),
            P(("tensor", "dp"), None),
            P(("tensor", "dp"), None),
            P(),
            P(),
            P(),
            P(),
            P(),
        ),
        check_vma=False,
    )
```

profile of v0, /device:TPU:0, one launch (start us, length us, event | category | flops | bytes accessed | tf_op | source)
XLA Modules:
  0.0 1104.4 jit_solution(1875028781626215786)
XLA Ops:
  16.8 36.3 %all_gather.26 = bf16[256,1024]{1,0:T(8,128)(2,1)} all-gather(bf16[32,1024]{1,0:T(8,128)(2,1)S(1)} %convert_element_type.159), channel_id=1, replica_groups=mesh['dp'=8,'tensor'=4] {'dp'}, dimensions={0}, use_global_device_ids=true | all-gather | bytes 589824 | tf_op jit(solution)/shard_map/all_gather | solution.py:120
  61.6 35.9 %all-gather.8.cloned.1.call-done = bf16[2048,1024]{1,0:T(8,128)(2,1)} async-done(((bf16[512,1024]{1,0:T(8,128)(2,1)}), bf16[2048,1024]{1,0:T(8,128)(2,1)}) %all-gather.8.cloned.1.call-update) | async-done | bytes 4194320 | tf_op jit(solution)/shard_map/all_gather | solution.py:132
  110.1 57.2 %while.47 = (s32[]{:T(128)}, bf16[4,512,4,64]{1,3,2,0:T(8,128)(2,1)}, f32[4,4,512,1]{2,1,3,0:T(4,128)}, s32[4,512]{1,0:T(4,128)S(1)}, s32[2048]{0:T(1024)S(1)}, ...) while((s32[]{:T(128)}, ...), condition=%wide.region_8.9_spmd, body=%wide.region_5.8_spmd.sunk | while | flops 1121056768 | bytes 57227380 | solution.py:163
  178.4 69.5 %reduce-scatter.8.cloned.1.call-done = f32[512,1024]{1,0:T(8,128)} async-done(((f32[2048,1024]{1,0:T(8,128)}), f32[512,1024]{1,0:T(8,128)}) %reduce-scatter.8.cloned.1.call-update) | async-done | bytes 2097168 | tf_op jit(solution)/shard_map/reduce_scatter | solution.py:173
  254.4 69.7 %all-gather.14.cloned.1.call-done = bf16[1024,2,1024]{2,1,0:T(2,128)(2,1)} async-done(((bf16[128,2,1024]{2,1,0:T(2,128)(2,1)}), bf16[1024,2,1024]{2,1,0:T(2,128)(2,1)}) %all-gather.14.cloned.1.call-update) | async-done | bytes 4194320 | tf_op jit(solution)/shard_map/all_gather | solution.py:121
  329.7 29.2 %all-gather.12.cloned.1.call-done = bf16[2048,1024]{1,0:T(8,128)(2,1)} async-done(((bf16[512,1024]{1,0:T(8,128)(2,1)}), bf16[2048,1024]{1,0:T(8,128)(2,1)}) %all-gather.12.cloned.1.call-update) | async-done | bytes 4194320 | tf_op jit(solution)/shard_map/all_gather | solution.py:180
  358.9 15.1 %fusion.96 = f32[2048,2048]{1,0:T(8,128)} fusion(bf16[2048,1024]{1,0:T(8,128)(2,1)} %all-gather.12.cloned.1.call-done, bf16[1024,2048]{1,0:T(8,128)(2,1)} %bitcast.176), kind=kOutput, calls=%fused_computation.180 | convolution fusion | flops 8589934592 | bytes 25165824 | tf_op jit(solution)/shard_map/dot_general | solution.py:181
  374.0 37.0 %all-gather.16.cloned.1.call-done = bf16[1024,1024]{1,0:T(8,128)(2,1)} async-done(((bf16[128,1024]{1,0:T(8,128)(2,1)}), bf16[1024,1024]{1,0:T(8,128)(2,1)}) %all-gather.16.cloned.1.call-update) | async-done | bytes 2097168 | tf_op jit(solution)/shard_map/all_gather | solution.py:122
  411.0 34.6 %all-gather.18.cloned.1.call-done = bf16[2048,1024]{1,0:T(8,128)(2,1)} async-done(((bf16[512,1024]{1,0:T(8,128)(2,1)}), bf16[2048,1024]{1,0:T(8,128)(2,1)}) %all-gather.18.cloned.1.call-update) | async-done | bytes 4194320 | tf_op jit(solution)/shard_map/all_gather | solution.py:191
  445.6 17.2 %fusion.73 = (f32[2048,1024]{1,0:T(8,128)}, f32[2048,1024]{1,0:T(8,128)}, bf16[2048,1024]{1,0:T(8,128)(2,1)}) fusion(f32[2048,2048]{1,0:T(8,128)} %fusion.96, bf16[2048,1024]{1,0:T(8,128)(2,1)} %all-gather.18.cloned.1.call-done, bf16[1024,1024]{1,0:T(8,128)(2,1)} %all-gather.16.cloned.1.call-done), kind=kOutput, calls=%fused_computation.124 | convolution fusion | flops 4324327424 | bytes 44040192 | tf_op jit(solution)/shard_map/dot_general | solution.py:85
  462.8 15.0 %convolution_convert_fusion.1 = bf16[2048,1024]{1,0:T(8,128)(2,1)} fusion(bf16[1024,2048]{1,0:T(8,128)(2,1)} %bitcast.177, f32[2048,1024]{1,0:T(8,128)} %get-tuple-element.338, f32[2048,1024]{1,0:T(8,128)} %get-tuple-element.337), kind=kOutput, calls=%fused_computation.65 | convolution fusion | flops 8600420352 | bytes 25165824 | tf_op jit(solution)/shard_map/dot_general | solution.py:85
  488.0 34.6 %reduce-scatter.12.cloned.1.call-done = bf16[512,1024]{1,0:T(8,128)(2,1)} async-done(((bf16[2048,1024]{1,0:T(8,128)(2,1)}), bf16[512,1024]{1,0:T(8,128)(2,1)}) %reduce-scatter.12.cloned.1.call-update) | async-done | bytes 1048592 | tf_op jit(solution)/shard_map/reduce_scatter | solution.py:196
  525.3 44.4 %reduce-scatter.10.cloned.1.call-done = bf16[512,1024]{1,0:T(8,128)(2,1)} async-done(((bf16[2048,1024]{1,0:T(8,128)(2,1)}), bf16[512,1024]{1,0:T(8,128)(2,1)}) %reduce-scatter.10.cloned.1.call-update) | async-done | bytes 1048592 | tf_op jit(solution)/shard_map/reduce_scatter | solution.py:183
  575.8 17.0 %convolution_convert_fusion = bf16[1024,2048]{1,0:T(8,128)(2,1)} fusion(bf16[2048,1024]{1,0:T(8,128)(2,1)} %all-gather.12.cloned.1.call-done, f32[2048,1024]{1,0:T(8,128)} %get-tuple-element.338, f32[2048,1024]{1,0:T(8,128)} %get-tuple-element.337), kind=kOutput, calls=%fused_computation.64 | convolution fusion | flops 8600420352 | bytes 25165824 | tf_op jit(solution)/shard_map/dot_general | solution.py:79
  620.5 230.1 %while.48 = (s32[]{:T(128)}, f32[2048,4,64]{0,2,1:T(8,128)}, f32[2048,4,64]{0,2,1:T(8,128)}, f32[4,512,4,64]{1,0,3,2:T(4,128)}, bf16[4,512,4,64]{1,3,2,0:T(8,128...) while((s32[]{:T(128)}, f32[2048,4,64]{0,2,1:T(8,128)}, ...), condition=%wide.region_18.19_spmd.clone, body=%wide.region_16.18_spmd.clone.sunk | while | flops 2751068160 | bytes 183179600 | solution.py:246
  632.8 11.5 %multiply_reduce_fusion.4 = (f32[4,512]{1,0:T(4,128)}, f32[4,512,2048]{2,1,0:T(8,128)}) fusion(f32[4,512,2048]{2,1,0:T(8,128)S(1)} %fusion.154, f32[4,512]{1,0:T(4,128)S(1)} %dynamic-slice_bitcast_fusion.2, pred[512,2048]{1,0:T(8,128)(4,1)} %copy-done.1, bf16[2048,4,64]{0,2,1:T(8,128)(2,1)} %get-tuple-element.552, ...), kind=kOutput, calls=%fused_computation.20.clone.1 | convolution fusion | flops 557840384 | bytes 35930116 | tf_op jit(solution)/shard_map/while/body/eval_jaxpr/while/body/eval_jaxpr/qhd,khd->hqk/dot_general | solution.py:218
  644.4 11.2 %multiply_convert_fusion.4 = bf16[4,512,2048]{2,1,0:T(8,128)(2,1)} fusion(f32[4,512,2048]{2,1,0:T(8,128)} %get-tuple-element.487, f32[4,512,2048]{2,1,0:T(8,128)S(1)} %fusion.154, f32[4,512]{1,0:T(4,128)} %get-tuple-element.488, f32[4,512]{1,0:T(4,128)S(1)} %dynamic-slice_bitcast_fusion.2, pred[512,2048]{1,0:T(8,128)(4,1)} %copy-done.1), kind=kLoop, calls=%fused_computation.19.clone.1 | loop fusion | flops 25165824 | bytes 43008000 | tf_op jit(solution)/shard_map/while/body/eval_jaxpr/while/body/eval_jaxpr/convert_element_type | solution.py:222
  689.9 11.5 %multiply_reduce_fusion.4 = (f32[4,512]{1,0:T(4,128)}, f32[4,512,2048]{2,1,0:T(8,128)}) fusion(f32[4,512,2048]{2,1,0:T(8,128)S(1)} %fusion.154, f32[4,512]{1,0:T(4,128)S(1)} %dynamic-slice_bitcast_fusion.2, pred[512,2048]{1,0:T(8,128)(4,1)} %copy-done.1, bf16[2048,4,64]{0,2,1:T(8,128)(2,1)} %get-tuple-element.552, ...), kind=kOutput, calls=%fused_computation.20.clone.1 | convolution fusion | flops 557840384 | bytes 35930116 | tf_op jit(solution)/shard_map/while/body/eval_jaxpr/while/body/eval_jaxpr/qhd,khd->hqk/dot_general | solution.py:218
  747.6 11.5 %multiply_reduce_fusion.4 = (f32[4,512]{1,0:T(4,128)}, f32[4,512,2048]{2,1,0:T(8,128)}) fusion(f32[4,512,2048]{2,1,0:T(8,128)S(1)} %fusion.154, f32[4,512]{1,0:T(4,128)S(1)} %dynamic-slice_bitcast_fusion.2, pred[512,2048]{1,0:T(8,128)(4,1)} %copy-done.1, bf16[2048,4,64]{0,2,1:T(8,128)(2,1)} %get-tuple-element.552, ...), kind=kOutput, calls=%fused_computation.20.clone.1 | convolution fusion | flops 557840384 | bytes 35930116 | tf_op jit(solution)/shard_map/while/body/eval_jaxpr/while/body/eval_jaxpr/qhd,khd->hqk/dot_general | solution.py:218
  805.3 11.5 %multiply_reduce_fusion.4 = (f32[4,512]{1,0:T(4,128)}, f32[4,512,2048]{2,1,0:T(8,128)}) fusion(f32[4,512,2048]{2,1,0:T(8,128)S(1)} %fusion.154, f32[4,512]{1,0:T(4,128)S(1)} %dynamic-slice_bitcast_fusion.2, pred[512,2048]{1,0:T(8,128)(4,1)} %copy-done.1, bf16[2048,4,64]{0,2,1:T(8,128)(2,1)} %get-tuple-element.552, ...), kind=kOutput, calls=%fused_computation.20.clone.1 | convolution fusion | flops 557840384 | bytes 35930116 | tf_op jit(solution)/shard_map/while/body/eval_jaxpr/while/body/eval_jaxpr/qhd,khd->hqk/dot_general | solution.py:218
  883.5 37.6 %reduce-scatter.18.cloned.1.call-done = bf16[32,1024]{1,0:T(8,128)(2,1)} async-done(((bf16[256,1024]{1,0:T(8,128)(2,1)}), bf16[32,1024]{1,0:T(8,128)(2,1)}) %reduce-scatter.18.cloned.1.call-update) | async-done | bytes 65552 | tf_op jit(solution)/shard_map/reduce_scatter | solution.py:278
  922.6 66.9 %reduce-scatter.16.cloned.1.call-done = bf16[128,3,256]{2,0,1:T(8,128)(2,1)} async-done(((bf16[1024,3,256]{2,0,1:T(8,128)(2,1)}), bf16[128,3,256]{2,0,1:T(8,128)(2,1)}) %reduce-scatter.16.cloned.1.call-update) | async-done | bytes 196624 | tf_op jit(solution)/shard_map/reduce_scatter | solution.py:272
  993.7 41.8 %reduce-scatter.14.cloned.1.call-done = bf16[512,1024]{1,0:T(8,128)(2,1)} async-done(((bf16[2048,1024]{1,0:T(8,128)(2,1)}), bf16[512,1024]{1,0:T(8,128)(2,1)}) %reduce-scatter.14.cloned.1.call-update) | async-done | bytes 1048592 | tf_op jit(solution)/shard_map/reduce_scatter | solution.py:263
  1039.7 39.7 %all-reduce.7 = (f32[]{:T(128)}, f32[2,1024]{1,0:T(2,128)S(1)}) all-reduce(f32[]{:T(128)S(6)} %add.210, f32[2,1024]{1,0:T(2,128)S(1)} %pad_maximum_fusion.1), channel_id=1, replica_groups=mesh['dp'=8,'tensor'=4] {'dp','tensor'}, use_global_device_ids=true, to_apply=%region_30.31 | all-reduce | flops 2049 | bytes 16392 | tf_op jit(solution)/shard_map/psum | solution.py:298
  (321 shorter events, 384.1 us)
Async XLA Ops:
  7.2 54.4 %all-gather.10.cloned.1.call-start = ((), (), s32[]{:S(2)}) async-start(), calls=%async_computation.8 | async-start | bytes 1769472 | tf_op jit(solution)/shard_map/all_gather | solution.py:119
  9.1 88.4 %all-gather.8.cloned.1.call-start = ((), (), s32[]{:S(2)}) async-start(), calls=%async_computation.7 | async-start | bytes 5242880 | tf_op jit(solution)/shard_map/all_gather | solution.py:132
  16.3 231.6 %reduce-scatter.8.cloned.1.call-start = ((), (), s32[]{:S(2)}) async-start(), calls=%async_computation.9 | async-start | bytes 10485760 | tf_op jit(solution)/shard_map/reduce_scatter | solution.py:173
  176.0 148.1 %all-gather.14.cloned.1.call-start = ((), (), s32[]{:S(2)}) async-start(), calls=%async_computation.11 | async-start | bytes 4718592 | tf_op jit(solution)/shard_map/all_gather | solution.py:121
  178.4 180.5 %all-gather.12.cloned.1.call-start = ((), (), s32[]{:S(2)}) async-start(), calls=%async_computation.10 | async-start | bytes 5242880 | tf_op jit(solution)/shard_map/all_gather | solution.py:180
  251.7 159.3 %all-gather.16.cloned.1.call-start = ((), (), s32[]{:S(2)}) async-start(), calls=%async_computation.12 | async-start | bytes 2359296 | tf_op jit(solution)/shard_map/all_gather | solution.py:122
  253.6 192.1 %all-gather.18.cloned.1.call-start = ((), (), s32[]{:S(2)}) async-start(), calls=%async_computation.14 | async-start | bytes 5242880 | tf_op jit(solution)/shard_map/all_gather | solution.py:191
  254.3 268.3 %reduce-scatter.12.cloned.1.call-start = ((), (), s32[]{:S(2)}) async-start(), calls=%async_computation.15 | async-start | bytes 5242880 | tf_op jit(solution)/shard_map/reduce_scatter | solution.py:196
  477.9 91.8 %reduce-scatter.10.cloned.1.call-start = ((), (), s32[]{:S(2)}) async-start(), calls=%async_computation.13 | async-start | bytes 5242880 | tf_op jit(solution)/shard_map/reduce_scatter | solution.py:183
  488.0 122.4 %all-gather.20.cloned.1.call-start = ((), (), s32[]{:S(2)}) async-start(), calls=%async_computation.16 | async-start | bytes 5242880 | tf_op jit(solution)/shard_map/all_gather | solution.py:204
  575.7 303.3 %all-reduce.10.cloned.1.call-start = ((), (), s32[]{:S(2)}) async-start(), calls=%async_computation.21 | async-start | bytes 8388608
  600.7 281.1 %reduce-scatter.20.cloned.1.call-start = ((), (), s32[]{:S(2)}) async-start(), calls=%async_computation.20 | async-start | bytes 2359296 | tf_op jit(solution)/shard_map/reduce_scatter | solution.py:287
  610.3 310.8 %reduce-scatter.18.cloned.1.call-start = ((), (), s32[]{:S(2)}) async-start(), calls=%async_computation.19 | async-start | bytes 589824 | tf_op jit(solution)/shard_map/reduce_scatter | solution.py:278
  858.7 130.7 %reduce-scatter.16.cloned.1.call-start = ((), (), s32[]{:S(2)}) async-start(), calls=%async_computation.18 | async-start | bytes 1769472 | tf_op jit(solution)/shard_map/reduce_scatter | solution.py:272
  870.1 165.4 %reduce-scatter.14.cloned.1.call-start = ((), (), s32[]{:S(2)}) async-start(), calls=%async_computation.17 | async-start | bytes 5242880 | tf_op jit(solution)/shard_map/reduce_scatter | solution.py:263
  877.2 158.3 %copy-start.41 = (f32[512]{0:T(512)S(1)}, f32[512]{0:T(512)}, u32[]{:S(2)}) copy-start(f32[512]{0:T(512)} %copy-done.40) | copy-start | bytes 6148
  877.2 160.1 %copy-start.48 = (f32[512]{0:T(512)S(1)}, f32[512]{0:T(512)}, u32[]{:S(2)}) copy-start(f32[512]{0:T(512)} %copy-done.47) | copy-start | bytes 6148
  877.2 160.1 %copy-start.44 = (f32[512]{0:T(512)S(1)}, f32[512]{0:T(512)}, u32[]{:S(2)}) copy-start(f32[512]{0:T(512)} %copy-done.43) | copy-start | bytes 6148
  877.2 162.5 %copy-start.49 = (f32[1024]{0:T(1024)S(1)}, f32[1024]{0:T(1024)}, u32[]{:S(2)}) copy-start(f32[1024]{0:T(1024)} %get-tuple-element.261) | copy-start | bytes 12292
  877.2 204.3 %copy-start.42 = (f32[2,1024]{1,0:T(2,128)S(1)}, f32[2,1024]{1,0:T(2,128)}, u32[]{:S(2)}) copy-start(f32[2,1024]{1,0:T(2,128)} %param.37) | copy-start | bytes 24580
  877.2 204.3 %copy-start.50 = (f32[2,1024]{1,0:T(2,128)S(1)}, f32[2,1024]{1,0:T(2,128)}, u32[]{:S(2)}) copy-start(f32[2,1024]{1,0:T(2,128)} %param.38) | copy-start | bytes 24580
  877.2 204.3 %copy-start.51 = (f32[2,1024]{1,0:T(2,128)S(1)}, f32[2,1024]{1,0:T(2,128)}, u32[]{:S(2)}) copy-start(f32[2,1024]{1,0:T(2,128)} %param.39) | copy-start | bytes 24580
  877.3 204.9 %copy-start.7 = (f32[512,1024]{1,0:T(8,128)S(1)}, f32[512,1024]{1,0:T(8,128)}, u32[]{:S(2)}) copy-start(f32[512,1024]{1,0:T(8,128)} %copy-done.6) | copy-start | bytes 6291460
  877.3 204.9 %copy-start.46 = (f32[512]{0:T(512)S(1)}, f32[512]{0:T(512)}, u32[]{:S(2)}) copy-start(f32[512]{0:T(512)} %copy-done.45) | copy-start | bytes 6148
  (65 other events, 810.9 us)
Sparse Core Ops, SparseCore 0:
  10.7 50.9 all-gather.9
  63.8 33.7 all-gather.7
  176.1 71.7 reduce-scatter.7
  250.6 73.3 all-gather.13
  326.1 32.7 all-gather.11
  361.7 49.2 all-gather.15
  412.6 32.9 all-gather.17
  478.0 44.5 reduce-scatter.11
  525.1 44.5 reduce-scatter.9
  575.9 34.4 all-gather.19
  614.5 156.3 all-reduce.9
  774.7 66.9 reduce-scatter.19
  858.9 62.1 reduce-scatter.17
  925.0 64.4 reduce-scatter.15
  992.0 43.4 reduce-scatter.13
where the time goes:
time: 1110 us; the launch traced here: 1100 us
  waiting for transfers between devices  510 us (46%)
  matrix products  283 us (25%)
  other arithmetic  125 us (11%)
  local copies, waits for them, and re-layouts  88.5 us (8%)
  blocking collectives  76 us (7%)
  between operations  20.7 us (2%)
    all_gather x1, waiting for transfers between devices, per_device(): lax.all_gather(in_master.astype(jnp.bfloat16), 'dp', axis=0, tiled=True)  69.7 us
    reduce_scatter x1, waiting for transfers between devices, per_device(): lax.psum_scatter(jnp.dot(attended, w_out, preferred_element_type=jnp.floa...  69.5 us
    reduce_scatter x1, waiting for transfers between devices, per_device(): lax.psum_scatter(grad_qkv.reshape(D, 3, width_local).astype(jnp.bfloat16)...  66.9 us
    dynamic_update_slice x8, local copies, waits for them, and re-layouts, backward_row(): lax.scan(backward_block, (zeros_acc, zeros_acc), block_inputs)  46.6 us
    dot_general x4, matrix products, backward_block(): jnp.einsum('qhd,khd->hqk', grad_block, value_row, preferred_element_type=...  46.1 us
    reduce_scatter x1, waiting for transfers between devices, per_device(): lax.psum_scatter(jnp.dot(hidden, w_down, preferred_element_type=jnp.float...  44.4 us
    convert_element_type x4, other arithmetic, backward_block(): score_grad = (probs_block * (prob_grad - row_inner)).astype(jnp.bfloat16)  44.2 us
    dot_general x4, matrix products, contract_cols(): lax.dot_general(left, right, (((1,), (1,)), ((), ())), preferred_element_...  43.7 us
  transfers between devices with their start and end apart: 15, of which 13 were waited for; matrix products, arithmetic and copies ran while one was open for 32% of the time, Pallas kernels for 0%

commit v1 on v0

--- a/solution.py
+++ b/solution.py
@@ -19,6 +19,28 @@
 weight_decay = 0.1
 adam_eps = 1e-08
 max_norm = 1.0
+
+
+def laid_out(blocks, dim):
+    blocks = jnp.moveaxis(blocks, 0, dim)
+    dims = blocks.shape
+    return blocks.reshape(*dims[:dim], dims[dim] * dims[dim + 1], *dims[dim + 2 :])
+
+
+def collected_by_bits(x, axis):
+    size = lax.axis_size(axis)
+    blocks = x[None]
+    for level in range(size.bit_length() - 1):
+        apart = 1 << level
+        other = lax.ppermute(blocks, axis, [(i, i ^ apart) for i in range(size)])
+        both = jnp.stack([blocks, other])
+        upper = lax.axis_index(axis) >> level & 1
+        blocks = jnp.where(upper == 0, both, both[::-1]).reshape(-1, *x.shape)
+    return blocks
+
+
+def collect(shard, axis, dim):
+    return laid_out(collected_by_bits(shard, axis), dim)
 
 
 def layer_norm(values, gain):
@@ -129,7 +151,7 @@
     gain_two = norm_gains[1]
     inputs = tokens.astype(jnp.float32)
     normed = layer_norm(inputs, gain_one)
-    gathered_one = lax.all_gather(normed.astype(jnp.bfloat16), "tensor", axis=0, tiled=True)
+    gathered_one = collect(normed.astype(jnp.bfloat16), "tensor", 0)
     projected = jnp.dot(gathered_one, w_qkv, preferred_element_type=jnp.float32)
     projected = projected.reshape(row_count, ROW, 3, heads_local, HEAD_DIM)
     queries = rotate(projected[:, :, 0], cosine, sine).astype(jnp.bfloat16)

time: 1110 us -> 1090 us (0.982)
  waiting for transfers between devices: 510 us -> 480 us
    all_gather x1 -> x0, waiting for transfers between devices: 35.9 us -> none  [per_device(): lax.all_gather(normed.astype(jnp.bfloat16), 'tensor', axis=0, tiled=True)]
    ppermute x0 -> x2, waiting for transfers between devices: none -> 11.9 us  [collected_by_bits(): other = lax.ppermute(blocks, axis, [(i, i ^ apart) for i in range(size)])]
  transfers between devices with their start and end apart: 15 -> 16, of which waited for: 13 -> 13; matrix products, arithmetic and copies ran while one was open for 32% -> 33% of each run, Pallas kernels for 0% -> 0%
where the time goes in v1:
time: 1090 us; the launch traced here: 1080 us
  waiting for transfers between devices  480 us (44%)
  matrix products  283 us (26%)
  other arithmetic  132 us (12%)
  local copies, waits for them, and re-layouts  86.9 us (8%)
  blocking collectives  74 us (7%)
  between operations  20.7 us (2%)
    reduce_scatter x1, waiting for transfers between devices, per_device(): lax.psum_scatter(jnp.dot(attended, w_out, preferred_element_type=jnp.floa...  70.9 us
    all_gather x1, waiting for transfers between devices, per_device(): lax.all_gather(in_master.astype(jnp.bfloat16), 'dp', axis=0, tiled=True)  70 us
    reduce_scatter x1, waiting for transfers between devices, per_device(): lax.psum_scatter(grad_qkv.reshape(D, 3, width_local).astype(jnp.bfloat16)...  67.1 us
    dynamic_update_slice x8, local copies, waits for them, and re-layouts, backward_row(): lax.scan(backward_block, (zeros_acc, zeros_acc), block_inputs)  46.6 us
    dot_general x4, matrix products, backward_block(): jnp.einsum('qhd,khd->hqk', grad_block, value_row, preferred_element_type=...  46.1 us
    reduce_scatter x1, waiting for transfers between devices, per_device(): lax.psum_scatter(jnp.dot(hidden, w_down, preferred_element_type=jnp.float...  44.4 us
    convert_element_type x4, other arithmetic, backward_block(): score_grad = (probs_block * (prob_grad - row_inner)).astype(jnp.bfloat16)  44.3 us
    dot_general x4, matrix products, contract_cols(): lax.dot_general(left, right, (((1,), (1,)), ((), ())), preferred_element_...  43.8 us
  transfers between devices with their start and end apart: 16, of which 13 were waited for; matrix products, arithmetic and copies ran while one was open for 33% of the time, Pallas kernels for 0%

profile of v1, /device:TPU:0, one launch (start us, length us, event | category | flops | bytes accessed | tf_op | source)
XLA Modules:
  0.0 1080.9 jit_solution(5650951755416345517)
XLA Ops:
  22.2 34.3 %all_gather.22 = bf16[256,1024]{1,0:T(8,128)(2,1)} all-gather(bf16[32,1024]{1,0:T(8,128)(2,1)S(1)} %convert_element_type.159), channel_id=1, replica_groups=mesh['dp'=8,'tensor'=4] {'dp'}, dimensions={0}, use_global_device_ids=true | all-gather | bytes 589824 | tf_op jit(solution)/shard_map/all_gather | solution.py:142
  85.0 57.2 %while.47 = (s32[]{:T(128)}, bf16[4,512,4,64]{1,3,2,0:T(8,128)(2,1)}, f32[4,4,512,1]{2,1,3,0:T(4,128)}, s32[4,512]{1,0:T(4,128)S(1)}, s32[2048]{0:T(1024)S(1)}, ...) while((s32[]{:T(128)}, ...), condition=%wide.region_8.9_spmd, body=%wide.region_5.8_spmd.sunk | while | flops 1121056768 | bytes 57227380 | solution.py:185
  153.3 70.9 %reduce-scatter.8.cloned.1.call-done = f32[512,1024]{1,0:T(8,128)} async-done(((f32[2048,1024]{1,0:T(8,128)}), f32[512,1024]{1,0:T(8,128)}) %reduce-scatter.8.cloned.1.call-update) | async-done | bytes 2097168 | tf_op jit(solution)/shard_map/reduce_scatter | solution.py:195
  230.6 70.0 %all-gather.11.cloned.1.call-done = bf16[1024,2,1024]{2,1,0:T(2,128)(2,1)} async-done(((bf16[128,2,1024]{2,1,0:T(2,128)(2,1)}), bf16[1024,2,1024]{2,1,0:T(2,128)(2,1)}) %all-gather.11.cloned.1.call-update) | async-done | bytes 4194320 | tf_op jit(solution)/shard_map/all_gather | solution.py:143
  306.2 29.2 %all-gather.9.cloned.1.call-done = bf16[2048,1024]{1,0:T(8,128)(2,1)} async-done(((bf16[512,1024]{1,0:T(8,128)(2,1)}), bf16[2048,1024]{1,0:T(8,128)(2,1)}) %all-gather.9.cloned.1.call-update) | async-done | bytes 4194320 | tf_op jit(solution)/shard_map/all_gather | solution.py:202
  335.4 15.1 %fusion.90 = f32[2048,2048]{1,0:T(8,128)} fusion(bf16[2048,1024]{1,0:T(8,128)(2,1)} %all-gather.9.cloned.1.call-done, bf16[1024,2048]{1,0:T(8,128)(2,1)} %bitcast.185), kind=kOutput, calls=%fused_computation.184 | convolution fusion | flops 8589934592 | bytes 25165824 | tf_op jit(solution)/shard_map/dot_general | solution.py:203
  350.5 37.0 %all-gather.13.cloned.1.call-done = bf16[1024,1024]{1,0:T(8,128)(2,1)} async-done(((bf16[128,1024]{1,0:T(8,128)(2,1)}), bf16[1024,1024]{1,0:T(8,128)(2,1)}) %all-gather.13.cloned.1.call-update) | async-done | bytes 2097168 | tf_op jit(solution)/shard_map/all_gather | solution.py:144
  387.5 34.5 %all-gather.15.cloned.1.call-done = bf16[2048,1024]{1,0:T(8,128)(2,1)} async-done(((bf16[512,1024]{1,0:T(8,128)(2,1)}), bf16[2048,1024]{1,0:T(8,128)(2,1)}) %all-gather.15.cloned.1.call-update) | async-done | bytes 4194320 | tf_op jit(solution)/shard_map/all_gather | solution.py:213
  422.0 17.2 %fusion.65 = (f32[2048,1024]{1,0:T(8,128)}, f32[2048,1024]{1,0:T(8,128)}, bf16[2048,1024]{1,0:T(8,128)(2,1)}) fusion(f32[2048,2048]{1,0:T(8,128)} %fusion.90, bf16[2048,1024]{1,0:T(8,128)(2,1)} %all-gather.15.cloned.1.call-done, bf16[1024,1024]{1,0:T(8,128)(2,1)} %all-gather.13.cloned.1.call-done), kind=kOutput, calls=%fused_computation.126 | convolution fusion | flops 4324327424 | bytes 44040192 | tf_op jit(solution)/shard_map/dot_general | solution.py:107
  439.2 15.1 %convolution_convert_fusion.1 = bf16[2048,1024]{1,0:T(8,128)(2,1)} fusion(bf16[1024,2048]{1,0:T(8,128)(2,1)} %bitcast.186, f32[2048,1024]{1,0:T(8,128)} %get-tuple-element.338, f32[2048,1024]{1,0:T(8,128)} %get-tuple-element.337), kind=kOutput, calls=%fused_computation.62 | convolution fusion | flops 8600420352 | bytes 25165824 | tf_op jit(solution)/shard_map/dot_general | solution.py:107
  464.4 34.6 %reduce-scatter.12.cloned.1.call-done = bf16[512,1024]{1,0:T(8,128)(2,1)} async-done(((bf16[2048,1024]{1,0:T(8,128)(2,1)}), bf16[512,1024]{1,0:T(8,128)(2,1)}) %reduce-scatter.12.cloned.1.call-update) | async-done | bytes 1048592 | tf_op jit(solution)/shard_map/reduce_scatter | solution.py:218
  501.7 44.4 %reduce-scatter.10.cloned.1.call-done = bf16[512,1024]{1,0:T(8,128)(2,1)} async-done(((bf16[2048,1024]{1,0:T(8,128)(2,1)}), bf16[512,1024]{1,0:T(8,128)(2,1)}) %reduce-scatter.10.cloned.1.call-update) | async-done | bytes 1048592 | tf_op jit(solution)/shard_map/reduce_scatter | solution.py:205
  552.1 17.0 %convolution_convert_fusion = bf16[1024,2048]{1,0:T(8,128)(2,1)} fusion(bf16[2048,1024]{1,0:T(8,128)(2,1)} %all-gather.9.cloned.1.call-done, f32[2048,1024]{1,0:T(8,128)} %get-tuple-element.338, f32[2048,1024]{1,0:T(8,128)} %get-tuple-element.337), kind=kOutput, calls=%fused_computation.61 | convolution fusion | flops 8600420352 | bytes 25165824 | tf_op jit(solution)/shard_map/dot_general | solution.py:101
  596.9 230.1 %while.48 = (s32[]{:T(128)}, f32[2048,4,64]{0,2,1:T(8,128)}, f32[2048,4,64]{0,2,1:T(8,128)}, f32[4,512,4,64]{1,0,3,2:T(4,128)}, bf16[4,512,4,64]{1,3,2,0:T(8,128...) while((s32[]{:T(128)}, f32[2048,4,64]{0,2,1:T(8,128)}, ...), condition=%wide.region_18.19_spmd.clone, body=%wide.region_16.18_spmd.clone.sunk | while | flops 2751068160 | bytes 183179600 | solution.py:268
  609.2 11.5 %multiply_reduce_fusion.4 = (f32[4,512]{1,0:T(4,128)}, f32[4,512,2048]{2,1,0:T(8,128)}) fusion(f32[4,512,2048]{2,1,0:T(8,128)S(1)} %fusion.150, f32[4,512]{1,0:T(4,128)S(1)} %dynamic-slice_bitcast_fusion.2, pred[512,2048]{1,0:T(8,128)(4,1)} %copy-done.1, bf16[2048,4,64]{0,2,1:T(8,128)(2,1)} %get-tuple-element.556, ...), kind=kOutput, calls=%fused_computation.20.clone.1 | convolution fusion | flops 557840384 | bytes 35930116 | tf_op jit(solution)/shard_map/while/body/eval_jaxpr/while/body/eval_jaxpr/qhd,khd->hqk/dot_general | solution.py:240
  620.7 11.1 %multiply_convert_fusion.4 = bf16[4,512,2048]{2,1,0:T(8,128)(2,1)} fusion(f32[4,512,2048]{2,1,0:T(8,128)} %get-tuple-element.491, f32[4,512,2048]{2,1,0:T(8,128)S(1)} %fusion.150, f32[4,512]{1,0:T(4,128)} %get-tuple-element.492, f32[4,512]{1,0:T(4,128)S(1)} %dynamic-slice_bitcast_fusion.2, pred[512,2048]{1,0:T(8,128)(4,1)} %copy-done.1), kind=kLoop, calls=%fused_computation.19.clone.1 | loop fusion | flops 25165824 | bytes 43008000 | tf_op jit(solution)/shard_map/while/body/eval_jaxpr/while/body/eval_jaxpr/convert_element_type | solution.py:244
  666.3 11.5 %multiply_reduce_fusion.4 = (f32[4,512]{1,0:T(4,128)}, f32[4,512,2048]{2,1,0:T(8,128)}) fusion(f32[4,512,2048]{2,1,0:T(8,128)S(1)} %fusion.150, f32[4,512]{1,0:T(4,128)S(1)} %dynamic-slice_bitcast_fusion.2, pred[512,2048]{1,0:T(8,128)(4,1)} %copy-done.1, bf16[2048,4,64]{0,2,1:T(8,128)(2,1)} %get-tuple-element.556, ...), kind=kOutput, calls=%fused_computation.20.clone.1 | convolution fusion | flops 557840384 | bytes 35930116 | tf_op jit(solution)/shard_map/while/body/eval_jaxpr/while/body/eval_jaxpr/qhd,khd->hqk/dot_general | solution.py:240
  700.3 11.1 %dynamic_update_slice.33 = f32[4,512,4,64]{1,0,3,2:T(4,128)} dynamic-update-slice(f32[4,512,4,64]{1,0,3,2:T(4,128)} %get-tuple-element.536, f32[1,512,4,64]{1,0,3,2:T(1,128)S(1)} %copy.107, s32[]{:T(128)S(6)} %copy.125, s32[]{:T(128)} %constant.73.clone.1..sunk, s32[]{:T(128)} %constant.73.clone.1..sunk, s32[]{:T(128)} %constant.73.clone.1..sunk) | dynamic-update-slice | bytes 1048580 | tf_op jit(solution)/shard_map/while/body/eval_jaxpr/while/body/jit(dynamic_update_index_in_dim)/dynamic_update_slice | solution.py:268
  724.0 11.5 %multiply_reduce_fusion.4 = (f32[4,512]{1,0:T(4,128)}, f32[4,512,2048]{2,1,0:T(8,128)}) fusion(f32[4,512,2048]{2,1,0:T(8,128)S(1)} %fusion.150, f32[4,512]{1,0:T(4,128)S(1)} %dynamic-slice_bitcast_fusion.2, pred[512,2048]{1,0:T(8,128)(4,1)} %copy-done.1, bf16[2048,4,64]{0,2,1:T(8,128)(2,1)} %get-tuple-element.556, ...), kind=kOutput, calls=%fused_computation.20.clone.1 | convolution fusion | flops 557840384 | bytes 35930116 | tf_op jit(solution)/shard_map/while/body/eval_jaxpr/while/body/eval_jaxpr/qhd,khd->hqk/dot_general | solution.py:240
  781.7 11.5 %multiply_reduce_fusion.4 = (f32[4,512]{1,0:T(4,128)}, f32[4,512,2048]{2,1,0:T(8,128)}) fusion(f32[4,512,2048]{2,1,0:T(8,128)S(1)} %fusion.150, f32[4,512]{1,0:T(4,128)S(1)} %dynamic-slice_bitcast_fusion.2, pred[512,2048]{1,0:T(8,128)(4,1)} %copy-done.1, bf16[2048,4,64]{0,2,1:T(8,128)(2,1)} %get-tuple-element.556, ...), kind=kOutput, calls=%fused_computation.20.clone.1 | convolution fusion | flops 557840384 | bytes 35930116 | tf_op jit(solution)/shard_map/while/body/eval_jaxpr/while/body/eval_jaxpr/qhd,khd->hqk/dot_general | solution.py:240
  860.0 37.5 %reduce-scatter.18.cloned.1.call-done = bf16[32,1024]{1,0:T(8,128)(2,1)} async-done(((bf16[256,1024]{1,0:T(8,128)(2,1)}), bf16[32,1024]{1,0:T(8,128)(2,1)}) %reduce-scatter.18.cloned.1.call-update) | async-done | bytes 65552 | tf_op jit(solution)/shard_map/reduce_scatter | solution.py:300
  898.9 67.1 %reduce-scatter.16.cloned.1.call-done = bf16[128,3,256]{2,0,1:T(8,128)(2,1)} async-done(((bf16[1024,3,256]{2,0,1:T(8,128)(2,1)}), bf16[128,3,256]{2,0,1:T(8,128)(2,1)}) %reduce-scatter.16.cloned.1.call-update) | async-done | bytes 196624 | tf_op jit(solution)/shard_map/reduce_scatter | solution.py:294
  970.2 41.8 %reduce-scatter.14.cloned.1.call-done = bf16[512,1024]{1,0:T(8,128)(2,1)} async-done(((bf16[2048,1024]{1,0:T(8,128)(2,1)}), bf16[512,1024]{1,0:T(8,128)(2,1)}) %reduce-scatter.14.cloned.1.call-update) | async-done | bytes 1048592 | tf_op jit(solution)/shard_map/reduce_scatter | solution.py:285
  1016.2 39.7 %all-reduce.7 = (f32[]{:T(128)}, f32[2,1024]{1,0:T(2,128)S(1)}) all-reduce(f32[]{:T(128)S(6)} %add.210, f32[2,1024]{1,0:T(2,128)S(1)} %pad_maximum_fusion.3), channel_id=1, replica_groups=mesh['dp'=8,'tensor'=4] {'dp','tensor'}, use_global_device_ids=true, to_apply=%region_30.31 | all-reduce | flops 2049 | bytes 16392 | tf_op jit(solution)/shard_map/psum | solution.py:320
  (328 shorter events, 385.7 us)
Async XLA Ops:
  7.2 65.2 %all-gather.7.cloned.1.call-start = ((), (), s32[]{:S(2)}) async-start(), calls=%async_computation.7 | async-start | bytes 1769472 | tf_op jit(solution)/shard_map/all_gather | solution.py:141
  12.8 2.8 collective-permute-start
  18.0 49.1 %collective-permute-start.1 = (bf16[2,512,1024]{2,1,0:T(8,128)(2,1)}, bf16[2,512,1024]{2,1,0:T(8,128)(2,1)}, u32[]{:S(2)}, u32[]{:S(2)}) collective-permute-start(bf16[2,512,1024]{2,1,0:T(8,128)(2,1)} %get-tuple-element.352), channel_id=1, source_target_pairs={{0,2},{1,3},{2,0},{3,1},{4,6},{5,7},{6,4},{7,5},{8,10},{9,11},{10,... | collective-permute-start | bytes 6291464 | tf_op jit(solution)/shard_map/ppermute | solution.py:35
  21.7 202.5 %reduce-scatter.8.cloned.1.call-start = ((), (), s32[]{:S(2)}) async-start(), calls=%async_computation.8 | async-start | bytes 10485760 | tf_op jit(solution)/shard_map/reduce_scatter | solution.py:195
  150.9 149.7 %all-gather.11.cloned.1.call-start = ((), (), s32[]{:S(2)}) async-start(), calls=%async_computation.10 | async-start | bytes 4718592 | tf_op jit(solution)/shard_map/all_gather | solution.py:143
  153.3 182.2 %all-gather.9.cloned.1.call-start = ((), (), s32[]{:S(2)}) async-start(), calls=%async_computation.9 | async-start | bytes 5242880 | tf_op jit(solution)/shard_map/all_gather | solution.py:202
  228.1 159.4 %all-gather.13.cloned.1.call-start = ((), (), s32[]{:S(2)}) async-start(), calls=%async_computation.11 | async-start | bytes 2359296 | tf_op jit(solution)/shard_map/all_gather | solution.py:144
  229.9 192.1 %all-gather.15.cloned.1.call-start = ((), (), s32[]{:S(2)}) async-start(), calls=%async_computation.13 | async-start | bytes 5242880 | tf_op jit(solution)/shard_map/all_gather | solution.py:213
  230.5 268.5 %reduce-scatter.12.cloned.1.call-start = ((), (), s32[]{:S(2)}) async-start(), calls=%async_computation.14 | async-start | bytes 5242880 | tf_op jit(solution)/shard_map/reduce_scatter | solution.py:218
  454.3 91.7 %reduce-scatter.10.cloned.1.call-start = ((), (), s32[]{:S(2)}) async-start(), calls=%async_computation.12 | async-start | bytes 5242880 | tf_op jit(solution)/shard_map/reduce_scatter | solution.py:205
  464.4 122.4 %all-gather.17.cloned.1.call-start = ((), (), s32[]{:S(2)}) async-start(), calls=%async_computation.15 | async-start | bytes 5242880 | tf_op jit(solution)/shard_map/all_gather | solution.py:226
  552.1 303.4 %all-reduce.10.cloned.1.call-start = ((), (), s32[]{:S(2)}) async-start(), calls=%async_computation.20 | async-start | bytes 8388608
  577.1 281.2 %reduce-scatter.20.cloned.1.call-start = ((), (), s32[]{:S(2)}) async-start(), calls=%async_computation.19 | async-start | bytes 2359296 | tf_op jit(solution)/shard_map/reduce_scatter | solution.py:309
  586.6 310.8 %reduce-scatter.18.cloned.1.call-start = ((), (), s32[]{:S(2)}) async-start(), calls=%async_computation.18 | async-start | bytes 589824 | tf_op jit(solution)/shard_map/reduce_scatter | solution.py:300
  835.2 130.8 %reduce-scatter.16.cloned.1.call-start = ((), (), s32[]{:S(2)}) async-start(), calls=%async_computation.17 | async-start | bytes 1769472 | tf_op jit(solution)/shard_map/reduce_scatter | solution.py:294
  846.5 165.5 %reduce-scatter.14.cloned.1.call-start = ((), (), s32[]{:S(2)}) async-start(), calls=%async_computation.16 | async-start | bytes 5242880 | tf_op jit(solution)/shard_map/reduce_scatter | solution.py:285
  853.6 160.1 %copy-start.50 = (f32[512]{0:T(512)S(1)}, f32[512]{0:T(512)}, u32[]{:S(2)}) copy-start(f32[512]{0:T(512)} %copy-done.49) | copy-start | bytes 6148
  853.6 160.2 %copy-start.46 = (f32[512]{0:T(512)S(1)}, f32[512]{0:T(512)}, u32[]{:S(2)}) copy-start(f32[512]{0:T(512)} %copy-done.45) | copy-start | bytes 6148
  853.6 162.6 %copy-start.51 = (f32[1024]{0:T(1024)S(1)}, f32[1024]{0:T(1024)}, u32[]{:S(2)}) copy-start(f32[1024]{0:T(1024)} %get-tuple-element.261) | copy-start | bytes 12292
  853.7 204.3 %copy-start.44 = (f32[2,1024]{1,0:T(2,128)S(1)}, f32[2,1024]{1,0:T(2,128)}, u32[]{:S(2)}) copy-start(f32[2,1024]{1,0:T(2,128)} %param.37) | copy-start | bytes 24580
  853.7 204.3 %copy-start.52 = (f32[2,1024]{1,0:T(2,128)S(1)}, f32[2,1024]{1,0:T(2,128)}, u32[]{:S(2)}) copy-start(f32[2,1024]{1,0:T(2,128)} %param.38) | copy-start | bytes 24580
  853.7 204.3 %copy-start.53 = (f32[2,1024]{1,0:T(2,128)S(1)}, f32[2,1024]{1,0:T(2,128)}, u32[]{:S(2)}) copy-start(f32[2,1024]{1,0:T(2,128)} %param.39) | copy-start | bytes 24580
  853.7 205.0 %copy-start.7 = (f32[512,1024]{1,0:T(8,128)S(1)}, f32[512,1024]{1,0:T(8,128)}, u32[]{:S(2)}) copy-start(f32[512,1024]{1,0:T(8,128)} %copy-done.6) | copy-start | bytes 6291460
  853.7 205.0 %copy-start.48 = (f32[512]{0:T(512)S(1)}, f32[512]{0:T(512)}, u32[]{:S(2)}) copy-start(f32[512]{0:T(512)} %copy-done.47) | copy-start | bytes 6148
  (67 other events, 908.1 us)
Sparse Core Ops, SparseCore 0:
  21.8 47.4 all-gather.6
  151.0 73.1 reduce-scatter.7
  227.2 73.3 all-gather.10
  302.7 32.7 all-gather.8
  338.2 49.2 all-gather.12
  389.0 32.9 all-gather.14
  454.4 44.5 reduce-scatter.11
  501.5 44.4 reduce-scatter.9
  552.2 34.4 all-gather.16
  590.7 156.3 all-reduce.9
  751.0 66.6 reduce-scatter.19
  835.3 62.0 reduce-scatter.17
  901.4 64.5 reduce-scatter.15
  968.5 43.4 reduce-scatter.13
